TPU v7x, 32 devices: a whole 2x2x4 slice. The times are simulated.
32 devices in a mesh: cols: 8 (over z, y), chan: 4 (over x, core).
Axes of the slice: x: 2, y: 2, z: 4, core: 2. Of those that a mesh axis runs over, the one named last changes fastest.
Arguments:
- anomaly: bfloat16 [2048, 80, 128], P('cols'), may hold values from -6 to 6
- jacobian: bfloat16 [1024, 256, 128], P(('cols', 'chan')), may hold values from -0.5 to 0.5
- foot_cols: int32 [1024, 4], P('cols'), may hold values from 0 to 2047, as said below
- foot_weight: float32 [1024, 4], P('cols'), may hold values from 0.1 to 1
- obs_count: int32 [8], P('cols'), may hold values from 32 to 128, as said below
- obs_weight: bfloat16 [256, 1024], P(None, ('cols', 'chan')), may hold values from 0.25 to 4
Outputs:
- radiance_pert: bfloat16 [80, 256, 1024], P(None, 'chan', 'cols')
- ensemble_gram: float32 [64, 80, 80], P('cols', 'chan')
Inputs may be any that keep to these rules, and one draw needn't show every extreme that they name: `foot_cols`: the footprint columns of an observation of tile t lie among the columns t * 256 - 32 to (t + 1) * 256 + 31, taken modulo 2048. The live observations of tile t are its first obs_count[t] slots; in every draw at least one tile has all 128 slots live.
All inputs are finite; a program needn't handle non-finite values.
Results may differ from a plain program's by a relative error of at most 0.0095.
Values may be sent and summed in bfloat16 or wider, within the bound.
A program may use at most 64 MiB of HBM per device.

v0:
```python
import jax
import jax.numpy as jnp
from jax import lax
from jax.sharding import PartitionSpec as P

CH = 256
OBS_DEV = 128
HALO = 32
PTS = 8


def extended_2(block, sides, width):
    for axis, dim in sides:
        count = lax.axis_size(axis)
        forward = [(i, i + 1) for i in range(count - 1)]
        forward.append((count - 1, 0))
        backward = [(target, source) for source, target in forward]
        low = lax.ppermute(
            lax.slice_in_dim(block, block.shape[dim] - width, None, axis=dim), axis, forward
        )
        high = lax.ppermute(lax.slice_in_dim(block, 0, width, axis=dim), axis, backward)
        block = jnp.concatenate([low, block, high], axis=dim)
    return block


def taper(distance, half_width):
    relative = jnp.abs(distance) / half_width
    near_part = (
        ((-0.25 * relative + 0.5) * relative + 0.625) * relative - 5.0 / 3.0
    ) * relative * relative + 1.0
    bounded = jnp.maximum(relative, 1.0)
    far_part = (
        ((((relative / 12.0 - 0.5) * relative + 0.625) * relative + 5.0 / 3.0) * relative - 5.0)
        * relative
        + 4.0
        - 2.0 / (3.0 * bounded)
    )
    return jnp.where(relative <= 1.0, near_part, jnp.where(relative <= 2.0, far_part, 0.0))


def local_gram(perturbed, error_weight, centers, tile_cols):
    spacing = tile_cols / PTS
    points = (jnp.arange(PTS, dtype=jnp.float32) + 0.5) * spacing
    locality = taper(centers[None, :] - points[:, None], spacing)
    weighted = perturbed.astype(jnp.float32) * error_weight.astype(jnp.float32)
    flat_values = perturbed.reshape(perturbed.shape[0], -1)
    gram_list = []
    for point_index in range(PTS):
        scaled = (weighted * locality[point_index][None, None, :]).astype(jnp.bfloat16)
        flat_scaled = scaled.reshape(perturbed.shape[0], -1)
        gram_list.append(
            jnp.einsum("mx,kx->mk", flat_scaled, flat_values, preferred_element_type=jnp.float32)
        )
    return jnp.stack(gram_list) / (CH * OBS_DEV)


def shards(anomaly, jacobian, foot_cols, foot_weight, obs_count, obs_weight):
    col_groups = lax.axis_size("cols")
    tile_index = lax.axis_index("cols")
    chan_index = lax.axis_index("chan")
    tile_cols = anomaly.shape[0]
    obs_share = jacobian.shape[0]
    extended = extended_2(anomaly, (("cols", 0),), HALO)
    offsets = jnp.mod(foot_cols - tile_index * tile_cols + HALO, tile_cols * col_groups)
    centers = jnp.sum(foot_weight * (offsets - HALO).astype(jnp.float32), axis=1) / jnp.sum(
        foot_weight, axis=1
    )
    first_obs = chan_index * obs_share
    own_offsets = lax.dynamic_slice_in_dim(offsets, first_obs, obs_share, 0)
    own_gains = lax.dynamic_slice_in_dim(foot_weight, first_obs, obs_share, 0)
    mixed_cols = jnp.zeros((obs_share, anomaly.shape[1], anomaly.shape[2]), jnp.float32)
    for column_slot in range(own_offsets.shape[1]):
        mixed_cols = mixed_cols + own_gains[:, column_slot, None, None] * extended[
            own_offsets[:, column_slot]
        ].astype(jnp.float32)
    mixed_cols = mixed_cols.astype(jnp.bfloat16)
    radiance = jnp.einsum("ncl,nml->mcn", jacobian, mixed_cols, preferred_element_type=jnp.float32)
    slot_numbers = first_obs + jnp.arange(obs_share, dtype=jnp.int32)
    live_mask = (slot_numbers < obs_count[0]).astype(jnp.float32)
    perturbed = (radiance * live_mask[None, None, :]).astype(jnp.bfloat16)
    error_weight = obs_weight[None]
    own_centers = lax.dynamic_slice_in_dim(centers, first_obs, obs_share, 0)
    partial_gram = local_gram(perturbed, error_weight, own_centers, tile_cols)
    received = lax.all_to_all(perturbed, "chan", split_axis=1, concat_axis=2, tiled=True)
    gram_rows = lax.psum_scatter(
        partial_gram.astype(jnp.bfloat16), "chan", scatter_dimension=1, tiled=True
    ).astype(jnp.float32)
    return (received, gram_rows)


def solution(mesh):
    return jax.shard_map(
        shards,
        mesh=mesh,
        in_specs=(
            P("cols", None, None),
            P(("cols", "chan"), None, None),
            P("cols", None),
            P("cols", None),
            P("cols"),
            P(None, ("cols", "chan")),
        ),
        out_specs=(P(None, "chan", "cols"), P("cols", "chan", None)),
        check_vma=False,
    )
```

profile of v0, /device:TPU:5, one launch (start us, length us, event | category | flops | bytes accessed | tf_op | source)
XLA Modules:
  0.0 119.4 jit_solution(7480939596906263955)
XLA Ops:
  7.2 1.5 %fusion.54 = (bf16[32,80,128]{2,1,0:T(8,128)(2,1)S(1)}, bf16[32,80,128]{2,1,0:T(8,128)(2,1)S(1)}) fusion(bf16[256,80,128]{2,1,0:T(8,128)(2,1)} %param.6), kind=kLoop, calls=%fused_computation.105 | loop fusion | bytes 2621440 | tf_op jit(solution)/shard_map/slice | solution.py:21
  8.7 1.3 %collective-permute-start = (bf16[32,80,128]{2,1,0:T(8,128)(2,1)S(1)}, bf16[32,80,128]{2,1,0:T(8,128)(2,1)}, u32[]{:S(2)}, u32[]{:S(2)}) collective-permute-start(bf16[32,80,128]{2,1,0:T(8,128)(2,1)S(1)} %get-tuple-element.12), channel_id=1, source_target_pairs={{0,4},{4,8},{8,12},{12,16},{16,20},{20,24},{24,28},{28,0},{1,5},{5... | collective-permute-start | bytes 1966088 | tf_op jit(solution)/shard_map/ppermute | solution.py:18
  10.0 0.2 collective-permute-start.1
  10.9 0.1 constant_dynamic-slice_fusion.1
  11.0 0.1 constant_dynamic-slice_fusion
  11.1 0.1 dynamic_slice.11
  11.2 0.1 fusion.46
  11.4 27.2 %collective-permute-done = bf16[32,80,128]{2,1,0:T(8,128)(2,1)} collective-permute-done((bf16[32,80,128]{2,1,0:T(8,128)(2,1)S(1)}, bf16[32,80,128]{2,1,0:T(8,128)(2,1)}, u32[]{:S(2)}, u32[]{:S(2)}) %collective-permute-start) | collective-permute-done | bytes 655392 | tf_op jit(solution)/shard_map/ppermute | solution.py:18
  38.5 2.0 %constant_dynamic-update-slice_fusion.2 = bf16[320,80,128]{2,1,0:T(8,128)(2,1)} fusion(bf16[32,80,128]{2,1,0:T(8,128)(2,1)} %collective-permute-done), kind=kLoop, calls=%fused_computation.63 | loop fusion | bytes 1310720
  40.5 5.7 %constant_dynamic-update-slice_fusion.1 = bf16[320,80,128]{2,1,0:T(8,128)(2,1)} fusion(bf16[320,80,128]{2,1,0:T(8,128)(2,1)} %constant_dynamic-update-slice_fusion.2, bf16[256,80,128]{2,1,0:T(8,128)(2,1)} %param.6), kind=kLoop, calls=%fused_computation.62 | loop fusion | bytes 10485760
  46.2 2.0 %constant_dynamic-update-slice_fusion = bf16[320,80,128]{2,1,0:T(8,128)(2,1)} fusion(bf16[320,80,128]{2,1,0:T(8,128)(2,1)} %constant_dynamic-update-slice_fusion.1, bf16[32,80,128]{2,1,0:T(8,128)(2,1)} %collective-permute-done.1), kind=kLoop, calls=%fused_computation.61 | loop fusion | bytes 1310720 | tf_op jit(solution)/shard_map/concatenate | solution.py:22
  48.2 4.3 %gather_fusion.3 = bf16[32,80,128]{2,1,0:T(8,128)(2,1)} fusion(bf16[320,80,128]{2,1,0:T(8,128)(2,1)} %constant_dynamic-update-slice_fusion, s32[1024]{0:T(1024)S(1)} %get-tuple-element.29), kind=kCustom, calls=%fused_computation.3 | custom fusion | bytes 1310848 | tf_op jit(solution)/shard_map/gather | solution.py:73
  52.5 4.4 %gather_fusion.2 = bf16[32,80,128]{2,1,0:T(8,128)(2,1)} fusion(bf16[320,80,128]{2,1,0:T(8,128)(2,1)} %constant_dynamic-update-slice_fusion, s32[1024]{0:T(1024)S(1)} %get-tuple-element.30), kind=kCustom, calls=%fused_computation.2 | custom fusion | bytes 1310848 | tf_op jit(solution)/shard_map/gather | solution.py:73
  56.9 4.3 %gather_fusion.1 = bf16[32,80,128]{2,1,0:T(8,128)(2,1)} fusion(bf16[320,80,128]{2,1,0:T(8,128)(2,1)} %constant_dynamic-update-slice_fusion, s32[1024]{0:T(1024)S(1)} %get-tuple-element.31), kind=kCustom, calls=%fused_computation.1 | custom fusion | bytes 1310848 | tf_op jit(solution)/shard_map/gather | solution.py:73
  61.2 4.4 %gather_fusion = bf16[32,80,128]{2,1,0:T(8,128)(2,1)} fusion(bf16[320,80,128]{2,1,0:T(8,128)(2,1)} %constant_dynamic-update-slice_fusion, s32[1024]{0:T(1024)S(1)} %get-tuple-element.32), kind=kCustom, calls=%fused_computation | custom fusion | bytes 1310848 | tf_op jit(solution)/shard_map/gather | solution.py:73
  65.6 2.6 %fusion.8 = bf16[80,256,32]{1,0,2:T(8,128)(2,1)S(1)} fusion(bf16[32,256,128]{2,1,0:T(8,128)(2,1)S(1)} %copy-done, f32[32]{0:T(128)S(1)} %compare_convert_fusion, bf16[32,80,128]{2,1,0:T(8,128)(2,1)} %gather_fusion.3, bf16[32,80,128]{2,1,0:T(8,128)(2,1)} %gather_fusion.2, bf16[32,80,128]{2,1,0:T(8,128)(2,1)} %gather_fusion.1, ...), kind=kOutput, calls=%fused_computation.22 | convolution fusion | flops 173015040 | bytes 6029952 | tf_op jit(solution)/shard_map/ncl,nml->mcn/dot_general | solution.py:77
  68.2 3.0 %copy.14 = bf16[80,256,32]{0,2,1:T(8,128)(2,1)} copy(bf16[80,256,32]{1,0,2:T(8,128)(2,1)S(1)} %fusion.8) | data formatting | bytes 2621440 | tf_op jit(solution)/shard_map/convert_element_type | solution.py:80
  71.2 5.9 %all-to-all-start = ((bf16[80,256,32]{0,2,1:T(8,128)(2,1)}), bf16[80,256,32]{0,2,1:T(8,128)(2,1)}, u32[]{:S(2)}, u32[]{:S(2)}) async-start(bf16[80,256,32]{0,2,1:T(8,128)(2,1)} %copy.14), calls=%async_computation | async-start | bytes 4194304 | tf_op jit(solution)/shard_map/all_to_all | solution.py:84
  77.2 0.6 fusion.40
  77.7 0.6 fusion.38
  78.3 0.6 fusion.36
  78.8 0.6 fusion.34
  79.4 0.6 fusion.32
  80.0 0.6 fusion.30
  80.5 0.6 fusion.28
  81.1 0.6 fusion.26
  81.7 0.7 copy.16
  82.4 0.0 reduce-scatter.2.cloned.1.call-update
  82.4 21.4 %reduce-scatter.2.cloned.1.call-done = bf16[8,20,80]{2,0,1:T(8,128)(2,1)} async-done(((bf16[8,80,80]{2,0,1:T(8,128)(2,1)}), bf16[8,20,80]{2,0,1:T(8,128)(2,1)}) %reduce-scatter.2.cloned.1.call-update) | async-done | bytes 25616 | tf_op jit(solution)/shard_map/reduce_scatter | solution.py:85
  103.8 1.4 %convert_element_type.88 = f32[8,20,80]{2,0,1:T(8,128)} convert(bf16[8,20,80]{2,0,1:T(8,128)(2,1)} %reduce-scatter.2.cloned.1.call-done) | non-fusion elementwise | flops 12800 | bytes 76800 | tf_op jit(solution)/shard_map/convert_element_type | solution.py:87
  105.2 3.6 %copy.15 = bf16[80,64,4,32]{0,3,2,1:T(8,128)(2,1)} copy(bf16[80,64,4,32]{0,3,1,2:T(8,128)(2,1)} %bitcast.11) | data formatting | bytes 2621440 | tf_op jit(solution)/shard_map/all_to_all | solution.py:84
  108.8 3.7 %copy.17 = bf16[80,64,128]{2,1,0:T(8,128)(2,1)} copy(bf16[80,64,128]{0,2,1:T(8,128)(2,1)} %bitcast.89) | data formatting | bytes 2621440
  (22 shorter events, 0.1 us)
Async XLA Ops:
  7.2 58.4 %copy-start = (bf16[32,256,128]{2,1,0:T(8,128)(2,1)S(1)}, bf16[32,256,128]{2,1,0:T(8,128)(2,1)}, u32[]{:S(2)}) copy-start(bf16[32,256,128]{2,1,0:T(8,128)(2,1)} %param.7) | copy-start | bytes 6291460
  7.2 3.7 %copy-start.2 = (f32[128,4]{0,1:T(4,128)S(1)}, f32[128,4]{0,1:T(4,128)}, u32[]{:S(2)}) copy-start(f32[128,4]{0,1:T(4,128)} %param.9) | copy-start | bytes 6148
  7.2 3.8 %copy-start.3 = (s32[128,4]{0,1:T(4,128)S(1)}, s32[128,4]{0,1:T(4,128)}, u32[]{:S(2)}) copy-start(s32[128,4]{0,1:T(4,128)} %param.8) | copy-start | bytes 6148
  7.2 4.0 %copy-start.1 = (bf16[256,32]{0,1:T(8,128)(2,1)S(1)}, bf16[256,32]{0,1:T(8,128)(2,1)}, u32[]{:S(2)}) copy-start(bf16[256,32]{0,1:T(8,128)(2,1)} %param.11) | copy-start | bytes 49156
  8.7 29.8 %collective-permute-start = (bf16[32,80,128]{2,1,0:T(8,128)(2,1)S(1)}, bf16[32,80,128]{2,1,0:T(8,128)(2,1)}, u32[]{:S(2)}, u32[]{:S(2)}) collective-permute-start(bf16[32,80,128]{2,1,0:T(8,128)(2,1)S(1)} %get-tuple-element.12), channel_id=1, source_target_pairs={{0,4},{4,8},{8,12},{12,16},{16,20},{20,24},{24,28},{28,0},{1,5},{5... | collective-permute-start | bytes 1966088 | tf_op jit(solution)/shard_map/ppermute | solution.py:18
  10.0 36.2 %collective-permute-start.1 = (bf16[32,80,128]{2,1,0:T(8,128)(2,1)S(1)}, bf16[32,80,128]{2,1,0:T(8,128)(2,1)}, u32[]{:S(2)}, u32[]{:S(2)}) collective-permute-start(bf16[32,80,128]{2,1,0:T(8,128)(2,1)S(1)} %get-tuple-element.11), channel_id=1, source_target_pairs={{4,0},{8,4},{12,8},{16,12},{20,16},{24,20},{28,24},{0,28},{5,1},{9... | collective-permute-start | bytes 1966088 | tf_op jit(solution)/shard_map/ppermute | solution.py:21
  71.2 34.0 %all-to-all-start = ((bf16[80,256,32]{0,2,1:T(8,128)(2,1)}), bf16[80,256,32]{0,2,1:T(8,128)(2,1)}, u32[]{:S(2)}, u32[]{:S(2)}) async-start(bf16[80,256,32]{0,2,1:T(8,128)(2,1)} %copy.14), calls=%async_computation | async-start | bytes 4194304 | tf_op jit(solution)/shard_map/all_to_all | solution.py:84
  77.2 26.6 %reduce-scatter.2.cloned.1.call-start = ((), (), s32[]{:S(2)}) async-start(), calls=%async_computation.2 | async-start | bytes 204800 | tf_op jit(solution)/shard_map/reduce_scatter | solution.py:85
Sparse Core Ops, SparseCore 0:
  82.5 21.2 reduce-scatter.1
where the time goes:
time: 121 us; the launch traced here: 119 us
  waiting for transfers between devices  48.6 us (40%)
  local copies, waits for them, and re-layouts  39.9 us (33%)
  between operations  14.8 us (12%)
  starting transfers between devices  7.46 us (6%)
  matrix products  7.01 us (6%)
  other arithmetic  1.61 us (1%)
    ppermute x1, waiting for transfers between devices, extended_2(): lax.ppermute(lax.slice_in_dim(block, block.shape[dim] - width, None, axis...  27.2 us
    reduce_scatter x1, waiting for transfers between devices, shards(): lax.psum_scatter(partial_gram.astype(jnp.bfloat16), 'chan', scatter_dimen...  21.4 us
    gather x4, local copies, waits for them, and re-layouts, shards(): extended[own_offsets[:, column_slot]].astype(jnp.float32)  17.4 us
    unnamed x11, local copies, waits for them, and re-layouts  11.4 us
    all_to_all x1, starting transfers between devices, shards(): lax.all_to_all(perturbed, 'chan', split_axis=1, concat_axis=2, tiled=True)  5.94 us
    dot_general x8, matrix products, local_gram(): jnp.einsum('mx,kx->mk', flat_scaled, flat_values, preferred_element_type=...  4.43 us
    all_to_all x1, local copies, waits for them, and re-layouts, shards(): lax.all_to_all(perturbed, 'chan', split_axis=1, concat_axis=2, tiled=True)  3.56 us
    convert_element_type x1, local copies, waits for them, and re-layouts, shards(): perturbed = (radiance * live_mask[None, None, :]).astype(jnp.bfloat16)  3.02 us
  transfers between devices with their start and end apart: 4, of which 2 were waited for; matrix products, arithmetic and copies ran while one was open for 12% of the time, Pallas kernels for 0%

commit v1 on v0

v1 whole, which is shorter than its diff:
```python
import functools

import jax
import jax.numpy as jnp
from jax import lax
from jax.experimental import pallas as pl
from jax.experimental.pallas import tpu as pltpu
from jax.sharding import PartitionSpec as P

HALO = 32
PTS = 8
LANES = 128
ROWS = 16
MESH = pl.DeviceIdType.MESH


def taper(distance, half_width):
    relative = jnp.abs(distance) / half_width
    near_part = (
        ((-0.25 * relative + 0.5) * relative + 0.625) * relative - 5.0 / 3.0
    ) * relative * relative + 1.0
    bounded = jnp.maximum(relative, 1.0)
    far_part = (
        ((((relative / 12.0 - 0.5) * relative + 0.625) * relative + 5.0 / 3.0) * relative - 5.0)
        * relative
        + 4.0
        - 2.0 / (3.0 * bounded)
    )
    return jnp.where(relative <= 1.0, near_part, jnp.where(relative <= 2.0, far_part, 0.0))


def kernel(
    ncols, nchan, anom, jac, fc_s, fw_s, cnt_s, fc_v, fw_v, ow_v, rad, gram, *scratch
):
    members = anom.shape[1]
    tile = anom.shape[0]
    obs, chans = jac.shape[0], jac.shape[1]
    slots = obs * nchan
    width = chans // nchan
    packs = LANES // width
    group = ROWS // packs
    chunks = members // ROWS
    rows = members // nchan
    foot = fc_v.shape[0]
    total = tile * ncols
    ext = scratch[:chunks]
    (jbuf, stage, sbuf, rbuf, rstore, wf, cent, loc, gs, gacc, gsend, grecv,
     sem_loc, sem_jac, sem_hs, sem_hr, sem_fs, sem_fr, sem_ss, sem_rs, sem_own,
     sem_gs, sem_gr) = scratch[chunks:]

    col = lax.axis_index("cols")
    chan = lax.axis_index("chan")
    core = lax.rem(chan, 2)
    partner = chan + 1 - 2 * core
    step = 1 - 2 * core
    ahead = lax.rem(col + step + ncols, ncols)
    behind = lax.rem(col - step + ncols, ncols)
    first = chan * obs

    barrier = pltpu.get_barrier_semaphore()
    for where in (ahead, behind):
        pl.semaphore_signal(barrier, inc=1, device_id=(where, chan), device_id_type=MESH)
    for d in range(1, nchan):
        pl.semaphore_signal(
            barrier, inc=1, device_id=(col, lax.rem(chan + d, nchan)), device_id_type=MESH
        )

    locals_ = []
    for k in range(chunks):
        copy = pltpu.make_async_copy(
            anom.at[:, pl.ds(k * ROWS, ROWS), :], ext[k].at[pl.ds(HALO, tile)], sem_loc.at[k]
        )
        copy.start()
        locals_.append(copy)
        if k == 0:
            jcopy = pltpu.make_async_copy(jac, jbuf, sem_jac.at[0])
            jcopy.start()

    pl.semaphore_wait(barrier, nchan + 1)
    src_col = (tile - HALO) * (1 - core)
    dst_col = (tile + HALO) * core
    halos = []
    for k in range(chunks):
        copy = pltpu.make_async_remote_copy(
            src_ref=anom.at[pl.ds(src_col, HALO), pl.ds(k * ROWS, ROWS), :],
            dst_ref=ext[k].at[pl.ds(dst_col, HALO)],
            send_sem=sem_hs.at[k],
            recv_sem=sem_hr.at[k],
            device_id=(ahead, chan),
            device_id_type=MESH,
        )
        copy.start()
        halos.append(copy)

    def offset_of(value):
        value = value - col * tile + HALO
        value = jnp.where(value < 0, value + total, value)
        return jnp.where(value >= total, value - total, value)

    gains = fw_v[...]
    offsets = (offset_of(fc_v[...]) - HALO).astype(jnp.float32)
    center = jnp.sum(gains * offsets, axis=0, keepdims=True) / jnp.sum(
        gains, axis=0, keepdims=True
    )
    cent[...] = jnp.transpose(jnp.broadcast_to(center, (LANES, slots)))
    mine = cent[pl.ds(pl.multiple_of(first, 8), obs), :]
    spacing = tile / PTS
    for p in range(PTS):
        loc[p] = taper(mine - (p + 0.5) * spacing, spacing) * (1.0 / (chans * slots))
    wf[...] = ow_v[...].astype(jnp.float32)

    lane = lax.broadcasted_iota(jnp.int32, (group, LANES), 1)
    live_count = cnt_s[0]
    jcopy.wait()

    sends = []
    for k in range(chunks):
        locals_[k].wait()
        halos[k].wait_recv()
        forward = pltpu.make_async_remote_copy(
            src_ref=ext[k].at[pl.ds(dst_col, HALO)],
            dst_ref=ext[k].at[pl.ds(dst_col, HALO)],
            send_sem=sem_fs.at[k],
            recv_sem=sem_fr.at[k],
            device_id=(col, partner),
            device_id_type=MESH,
        )
        forward.start()
        forward.wait_recv()

        def one(n, carry, k=k):
            slot = first + n
            mixed = None
            for f in range(foot):
                at = jnp.minimum(offset_of(fc_s[f, slot]), tile + 2 * HALO - 1)
                at = jnp.maximum(at, 0)
                part = fw_s[f, slot] * ext[k][at].astype(jnp.float32)
                mixed = part if mixed is None else mixed + part
            live = jnp.where(slot < live_count, 1.0, 0.0).astype(jnp.float32)
            radiance = lax.dot_general(
                mixed.astype(jnp.bfloat16), jbuf[n], (((1,), (1,)), ((), ())),
                preferred_element_type=jnp.float32,
            ) * live
            rstore[n, k * ROWS:(k + 1) * ROWS, :] = radiance.astype(jnp.bfloat16)
            for q in range(nchan):
                start = q * width
                block, shift = start // LANES * LANES, start % LANES
                piece = None
                for h in range(packs):
                    part = radiance[h * group:(h + 1) * group, block:block + LANES]
                    turn = (h * width - shift) % LANES
                    if turn:
                        part = pltpu.roll(part, turn, 1)
                    piece = part if piece is None else jnp.where(lane < h * width, piece, part)
                stage[q, pl.ds(n, group, stride=obs), :] = piece
            return carry

        lax.fori_loop(0, obs, one, 0, unroll=4)
        for q in range(nchan):
            sbuf[k, q] = stage[q].astype(jnp.bfloat16).reshape(group, obs, LANES)
        place = pl.ds(pl.multiple_of(first, obs), obs)
        for d in range(1, nchan):
            to = lax.rem(chan + d, nchan)
            copy = pltpu.make_async_remote_copy(
                src_ref=sbuf.at[k, to],
                dst_ref=rbuf.at[k, :, place, :],
                send_sem=sem_ss.at[k, d],
                recv_sem=sem_rs.at[k, d],
                device_id=(col, to),
                device_id_type=MESH,
            )
            copy.start()
            sends.append((k, copy))
        own = pltpu.make_async_copy(sbuf.at[k, chan], rbuf.at[k, :, place, :], sem_own.at[k])
        own.start()
        sends.append((k, own))
        forward.wait_send()
        halos[k].wait_send()

    def product(n, carry):
        values = rstore[n]
        weighted = (values.astype(jnp.float32) * wf[pl.ds(n, 1), :]).astype(jnp.bfloat16)
        gs[n] = lax.dot_general(
            weighted, values, (((1,), (1,)), ((), ())), preferred_element_type=jnp.float32
        )
        return carry

    lax.fori_loop(0, obs, product, 0, unroll=4)

    def point(p, carry):
        sums = [None, None]
        for n in range(obs):
            value = gs[n]
            for i in range(2):
                part = loc[2 * p + i, pl.ds(n, 1), :][:, :members] * value
                sums[i] = part if sums[i] is None else sums[i] + part
        for i in range(2):
            gacc[2 * p + i] = sums[i]
        return carry

    lax.fori_loop(0, PTS // 2, point, 0)
    for q in range(nchan):
        gsend[q] = gacc[:, q * rows:(q + 1) * rows, :].astype(jnp.bfloat16)
    gsends = []
    for d in range(1, nchan):
        to = lax.rem(chan + d, nchan)
        copy = pltpu.make_async_remote_copy(
            src_ref=gsend.at[to],
            dst_ref=grecv.at[d],
            send_sem=sem_gs.at[d],
            recv_sem=sem_gr.at[d],
            device_id=(col, to),
            device_id_type=MESH,
        )
        copy.start()
        gsends.append(copy)

    for k in range(chunks):
        for at, copy in sends:
            if at == k:
                copy.wait()

        def turn_one(j, carry, k=k):
            turned = jnp.transpose(rbuf[k, j].astype(jnp.float32)).astype(jnp.bfloat16)
            for h in range(packs):
                rad[k * ROWS + h * group + j] = turned[h * width:(h + 1) * width]
            return carry

        lax.fori_loop(0, group, turn_one, 0, unroll=2)

    result = gsend[chan].astype(jnp.float32)
    for d in range(1, nchan):
        gsends[d - 1].wait()
        result = result + grecv[d].astype(jnp.float32)
    gram[...] = result


def shards(ncols, nchan, anomaly, jacobian, foot_cols, foot_weight, obs_count, obs_weight):
    tile, members, levels = anomaly.shape
    obs, chans = jacobian.shape[:2]
    slots, foot = foot_cols.shape
    width = chans // nchan
    group = ROWS // (LANES // width)
    chunks = members // ROWS
    rows = members // nchan
    cols_t, gains_t = foot_cols.T, foot_weight.T
    vmem = pl.BlockSpec(memory_space=pltpu.VMEM)
    smem = pl.BlockSpec(memory_space=pltpu.SMEM)
    anyspace = pl.BlockSpec(memory_space=pl.ANY)
    dma = pltpu.SemaphoreType.DMA
    return pl.pallas_call(
        functools.partial(kernel, ncols, nchan),
        out_shape=(
            jax.ShapeDtypeStruct((members, width, slots), jnp.bfloat16),
            jax.ShapeDtypeStruct((PTS, rows, members), jnp.float32),
        ),
        in_specs=[anyspace, anyspace, smem, smem, smem, vmem, vmem, vmem],
        out_specs=(vmem, vmem),
        scratch_shapes=[
            *[pltpu.VMEM((tile + 2 * HALO, ROWS, levels), jnp.bfloat16) for _ in range(chunks)],
            pltpu.VMEM((obs, chans, levels), jnp.bfloat16),
            pltpu.VMEM((nchan, group * obs, LANES), jnp.float32),
            pltpu.VMEM((chunks, nchan, group, obs, LANES), jnp.bfloat16),
            pltpu.VMEM((chunks, group, slots, LANES), jnp.bfloat16),
            pltpu.VMEM((obs, members, chans), jnp.bfloat16),
            pltpu.VMEM((obs, chans), jnp.float32),
            pltpu.VMEM((slots, LANES), jnp.float32),
            pltpu.VMEM((PTS, obs, LANES), jnp.float32),
            pltpu.VMEM((obs, members, members), jnp.float32),
            pltpu.VMEM((PTS, members, members), jnp.float32),
            pltpu.VMEM((nchan, PTS, rows, members), jnp.bfloat16),
            pltpu.VMEM((nchan, PTS, rows, members), jnp.bfloat16),
            dma((chunks,)),
            dma((1,)),
            dma((chunks,)),
            dma((chunks,)),
            dma((chunks,)),
            dma((chunks,)),
            dma((chunks, nchan)),
            dma((chunks, nchan)),
            dma((chunks,)),
            dma((nchan,)),
            dma((nchan,)),
        ],
        compiler_params=pltpu.CompilerParams(
            collective_id=0, has_side_effects=True, vmem_limit_bytes=48 * 1024 * 1024
        ),
    )(anomaly, jacobian, cols_t, gains_t, obs_count, cols_t, gains_t, obs_weight.T)


def solution(mesh):
    return jax.shard_map(
        functools.partial(shards, mesh.shape["cols"], mesh.shape["chan"]),
        mesh=mesh,
        in_specs=(
            P("cols", None, None),
            P(("cols", "chan"), None, None),
            P("cols", None),
            P("cols", None),
            P("cols"),
            P(None, ("cols", "chan")),
        ),
        out_specs=(P(None, "chan", "cols"), P("cols", "chan", None)),
        check_vma=False,
    )
```

time: 121 us -> 44.9 us (0.37); the launches traced: 119 us -> 44.6 us
  waiting for transfers between devices: 48.6 us -> 0 us
  Pallas kernels: 0 us -> 38 us
  local copies, waits for them, and re-layouts: 39.9 us -> 5.37 us
  between operations: 14.8 us -> 1.3 us
  starting transfers between devices: 7.46 us -> 0 us
  matrix products: 7.01 us -> 0 us
  other arithmetic: 1.61 us -> 0 us
    pallas_call x0 -> x1, Pallas kernels: none -> 38 us  [shards(): pl.pallas_call(functools.partial(kernel, ncols, nchan), out_shape=(jax.Sh...]
    ppermute x2 -> x0, waiting for transfers between devices: 27.2 us -> none  [the longest x1 27.2 us: extended_2(): lax.ppermute(lax.slice_in_dim(block, block.shape[dim] - width, None, axis...]
    reduce_scatter x1 -> x0, waiting for transfers between devices: 21.4 us -> none  [shards(): lax.psum_scatter(partial_gram.astype(jnp.bfloat16), 'chan', scatter_dimen...]
    gather x4 -> x0, local copies, waits for them, and re-layouts: 17.4 us -> none  [shards(): extended[own_offsets[:, column_slot]].astype(jnp.float32)]
    dot_general x9 -> x0, matrix products: 7.01 us -> none  [the longest x8 4.43 us: local_gram(): jnp.einsum('mx,kx->mk', flat_scaled, flat_values, preferred_element_type=...]
    unnamed x11 -> x9, local copies, waits for them, and re-layouts: 11.4 us -> 4.72 us
    all_to_all x1 -> x0, starting transfers between devices: 5.94 us -> none  [shards(): lax.all_to_all(perturbed, 'chan', split_axis=1, concat_axis=2, tiled=True)]
    convert_element_type x2 -> x0, local copies, waits for them, and re-layouts: 3.73 us -> none  [the longest x1 3.02 us: shards(): perturbed = (radiance * live_mask[None, None, :]).astype(jnp.bfloat16)]
  transfers between devices with their start and end apart: 4 -> 0, of which waited for: 2 -> 0; matrix products, arithmetic and copies ran while one was open for 12% -> 0% of each run, Pallas kernels for 0% -> 0%
where the time goes in v1:
time: 44.9 us; the launch traced here: 44.6 us
  Pallas kernels  38 us (85%)
  local copies, waits for them, and re-layouts  5.37 us (12%)
  between operations  1.3 us (3%)
    pallas_call x1, Pallas kernels, shards(): pl.pallas_call(functools.partial(kernel, ncols, nchan), out_shape=(jax.Sh...  38 us
    unnamed x9, local copies, waits for them, and re-layouts  4.72 us

profile of v1, /device:TPU:5, one launch (start us, length us, event | category | flops | bytes accessed | tf_op | source)
XLA Modules:
  0.0 44.6 jit_solution(12588870549584314421)
XLA Ops:
  1.3 0.0 copy-start
  1.3 1.6 %copy-done = bf16[32,256,128]{2,1,0:T(8,128)(2,1)S(1)} copy-done((bf16[32,256,128]{2,1,0:T(8,128)(2,1)S(1)}, bf16[32,256,128]{2,1,0:T(8,128)(2,1)}, u32[]{:S(2)}) %copy-start) | copy-done | bytes 2097176
  2.9 0.0 copy-start.1
  2.9 0.7 %copy-done.1 = bf16[256,32]{0,1:T(8,128)(2,1)S(1)} copy-done((bf16[256,32]{0,1:T(8,128)(2,1)S(1)}, bf16[256,32]{0,1:T(8,128)(2,1)}, u32[]{:S(2)}) %copy-start.1) | copy-done | bytes 16408
  3.6 0.0 copy-start.2
  3.6 0.7 %copy-done.2 = s32[128,4]{0,1:T(4,128)S(1)} copy-done((s32[128,4]{0,1:T(4,128)S(1)}, s32[128,4]{0,1:T(4,128)}, u32[]{:S(2)}) %copy-start.2) | copy-done | bytes 2072
  4.3 0.0 copy-start.3
  4.3 0.7 %copy-done.3 = f32[128,4]{0,1:T(4,128)S(1)} copy-done((f32[128,4]{0,1:T(4,128)S(1)}, f32[128,4]{0,1:T(4,128)}, u32[]{:S(2)}) %copy-start.3) | copy-done | bytes 2072
  5.0 38.0 %shard_map.77 = (bf16[80,64,128]{2,1,0:T(8,128)(2,1)S(1)}, f32[8,20,80]{2,1,0:T(8,128)S(1)}) custom-call(bf16[256,80,128]{2,1,0:T(8,128)(2,1)} %anom.1, bf16[32,256,128]{2,1,0:T(8,128)(2,1)S(1)} %copy-done, s32[4,128]{1,0:T(4,128)S(1)} %bitcast.4, f32[4,128]{1,0:T(4,128)S(1)} %bitcast.6, s32[1]{0:T(128)S(6)} %copy.10.cnt_s, s32[4,128]{1,0:T(4,128)S(1)} %bitcast.5, ...), custom_call_target="tpu_custom_call" | custom-call | tf_op jit(solution)/shard_map/pallas_call | solution.py:251
  42.9 0.7 %copy.8 = f32[8,20,80]{2,0,1:T(8,128)} copy(f32[8,20,80]{2,1,0:T(8,128)S(1)} %get-tuple-element.3) | data formatting | bytes 102400 | tf_op jit(solution)/shard_map/pallas_call | solution.py:251
  43.6 1.1 %copy.11 = bf16[80,64,128]{2,1,0:T(8,128)(2,1)} copy(bf16[80,64,128]{2,1,0:T(8,128)(2,1)S(1)} %get-tuple-element.6) | data formatting | bytes 2621440
Async XLA Ops:
  1.3 1.6 %copy-start = (bf16[32,256,128]{2,1,0:T(8,128)(2,1)S(1)}, bf16[32,256,128]{2,1,0:T(8,128)(2,1)}, u32[]{:S(2)}) copy-start(bf16[32,256,128]{2,1,0:T(8,128)(2,1)} %jac.1) | copy-start | bytes 6291460
  2.9 0.7 %copy-start.1 = (bf16[256,32]{0,1:T(8,128)(2,1)S(1)}, bf16[256,32]{0,1:T(8,128)(2,1)}, u32[]{:S(2)}) copy-start(bf16[256,32]{0,1:T(8,128)(2,1)} %param.11) | copy-start | bytes 49156
  3.6 0.7 %copy-start.2 = (s32[128,4]{0,1:T(4,128)S(1)}, s32[128,4]{0,1:T(4,128)}, u32[]{:S(2)}) copy-start(s32[128,4]{0,1:T(4,128)} %param.8) | copy-start | bytes 6148
  4.3 0.7 %copy-start.3 = (f32[128,4]{0,1:T(4,128)S(1)}, f32[128,4]{0,1:T(4,128)}, u32[]{:S(2)}) copy-start(f32[128,4]{0,1:T(4,128)} %param.9) | copy-start | bytes 6148

commit v2 on v1

--- a/solution.py
+++ b/solution.py
@@ -30,7 +30,7 @@
 
 
 def kernel(
-    ncols, nchan, anom, jac, fc_s, fw_s, cnt_s, fc_v, fw_v, ow_v, rad, gram, *scratch
+    ncols, nchan, anom, jac, fc_h, fw_h, ow_h, cnt_s, rad, gram, *scratch
 ):
     members = anom.shape[1]
     tile = anom.shape[0]
@@ -41,12 +41,12 @@
     group = ROWS // packs
     chunks = members // ROWS
     rows = members // nchan
-    foot = fc_v.shape[0]
+    foot = fc_h.shape[0]
     total = tile * ncols
     ext = scratch[:chunks]
     (jbuf, stage, sbuf, rbuf, rstore, wf, cent, loc, gs, gacc, gsend, grecv,
      sem_loc, sem_jac, sem_hs, sem_hr, sem_fs, sem_fr, sem_ss, sem_rs, sem_own,
-     sem_gs, sem_gr) = scratch[chunks:]
+     sem_gs, sem_gr, fc_s, fw_s, fc_v, fw_v, ow_v, sem_in) = scratch[chunks:]
 
     col = lax.axis_index("cols")
     chan = lax.axis_index("chan")
@@ -65,16 +65,13 @@
             barrier, inc=1, device_id=(col, lax.rem(chan + d, nchan)), device_id_type=MESH
         )
 
-    locals_ = []
-    for k in range(chunks):
-        copy = pltpu.make_async_copy(
-            anom.at[:, pl.ds(k * ROWS, ROWS), :], ext[k].at[pl.ds(HALO, tile)], sem_loc.at[k]
-        )
-        copy.start()
-        locals_.append(copy)
-        if k == 0:
-            jcopy = pltpu.make_async_copy(jac, jbuf, sem_jac.at[0])
-            jcopy.start()
+    inputs = []
+    for i, (source, target) in enumerate(
+        ((fc_h, fc_v), (fw_h, fw_v), (fc_h, fc_s), (fw_h, fw_s), (ow_h, ow_v))
+    ):
+        copy = pltpu.make_async_copy(source, target, sem_in.at[i])
+        copy.start()
+        inputs.append(copy)
 
     pl.semaphore_wait(barrier, nchan + 1)
     src_col = (tile - HALO) * (1 - core)
@@ -92,6 +89,20 @@
         copy.start()
         halos.append(copy)
 
+    locals_ = []
+    for k in range(chunks):
+        copy = pltpu.make_async_copy(
+            anom.at[:, pl.ds(k * ROWS, ROWS), :], ext[k].at[pl.ds(HALO, tile)], sem_loc.at[k]
+        )
+        copy.start()
+        locals_.append(copy)
+        if k == 0:
+            jcopy = pltpu.make_async_copy(jac, jbuf, sem_jac.at[0])
+            jcopy.start()
+
+    for copy in inputs:
+        copy.wait()
+
     def offset_of(value):
         value = value - col * tile + HALO
         value = jnp.where(value < 0, value + total, value)
@@ -113,11 +124,11 @@
     live_count = cnt_s[0]
     jcopy.wait()
 
-    sends = []
-    for k in range(chunks):
-        locals_[k].wait()
+    forwards = []
+
+    def pass_on(k):
         halos[k].wait_recv()
-        forward = pltpu.make_async_remote_copy(
+        copy = pltpu.make_async_remote_copy(
             src_ref=ext[k].at[pl.ds(dst_col, HALO)],
             dst_ref=ext[k].at[pl.ds(dst_col, HALO)],
             send_sem=sem_fs.at[k],
@@ -125,8 +136,16 @@
             device_id=(col, partner),
             device_id_type=MESH,
         )
-        forward.start()
-        forward.wait_recv()
+        copy.start()
+        forwards.append(copy)
+
+    sends = []
+    pass_on(0)
+    for k in range(chunks):
+        if k + 1 < chunks:
+            pass_on(k + 1)
+        locals_[k].wait()
+        forwards[k].wait_recv()
 
         def one(n, carry, k=k):
             slot = first + n
@@ -174,7 +193,7 @@
         own = pltpu.make_async_copy(sbuf.at[k, chan], rbuf.at[k, :, place, :], sem_own.at[k])
         own.start()
         sends.append((k, own))
-        forward.wait_send()
+        forwards[k].wait_send()
         halos[k].wait_send()
 
     def product(n, carry):
@@ -243,10 +262,8 @@
     group = ROWS // (LANES // width)
     chunks = members // ROWS
     rows = members // nchan
-    cols_t, gains_t = foot_cols.T, foot_weight.T
     vmem = pl.BlockSpec(memory_space=pltpu.VMEM)
-    smem = pl.BlockSpec(memory_space=pltpu.SMEM)
-    anyspace = pl.BlockSpec(memory_space=pl.ANY)
+    hbm = pl.BlockSpec(memory_space=pltpu.HBM)
     dma = pltpu.SemaphoreType.DMA
     return pl.pallas_call(
         functools.partial(kernel, ncols, nchan),
@@ -254,7 +271,7 @@
             jax.ShapeDtypeStruct((members, width, slots), jnp.bfloat16),
             jax.ShapeDtypeStruct((PTS, rows, members), jnp.float32),
         ),
-        in_specs=[anyspace, anyspace, smem, smem, smem, vmem, vmem, vmem],
+        in_specs=[*[hbm] * 5, pl.BlockSpec(memory_space=pltpu.SMEM)],
         out_specs=(vmem, vmem),
         scratch_shapes=[
             *[pltpu.VMEM((tile + 2 * HALO, ROWS, levels), jnp.bfloat16) for _ in range(chunks)],
@@ -281,11 +298,23 @@
             dma((chunks,)),
             dma((nchan,)),
             dma((nchan,)),
+            pltpu.SMEM((foot, slots), jnp.int32),
+            pltpu.SMEM((foot, slots), jnp.float32),
+            pltpu.VMEM((foot, slots), jnp.int32),
+            pltpu.VMEM((foot, slots), jnp.float32),
+            pltpu.VMEM((obs, chans), jnp.bfloat16),
+            dma((5,)),
         ],
         compiler_params=pltpu.CompilerParams(
             collective_id=0, has_side_effects=True, vmem_limit_bytes=48 * 1024 * 1024
         ),
-    )(anomaly, jacobian, cols_t, gains_t, obs_count, cols_t, gains_t, obs_weight.T)
+    )(
+        *(
+            pltpu.with_memory_space_constraint(x, pltpu.HBM)
+            for x in (anomaly, jacobian, foot_cols.T, foot_weight.T, obs_weight.T)
+        ),
+        obs_count,
+    )
 
 
 def solution(mesh):

time: 44.9 us -> 38.2 us (0.85)
  local copies, waits for them, and re-layouts: 5.37 us -> 1.71 us
  Pallas kernels: 38 us -> 35.1 us
    unnamed x9 -> x1, local copies, waits for them, and re-layouts: 4.72 us -> 1.06 us
    pallas_call x1, Pallas kernels: 38 us -> 35.1 us  [shards(): pl.pallas_call(functools.partial(kernel, ncols, nchan), out_shape=(jax.Sh...]
where the time goes in v2:
time: 38.2 us; the launch traced here: 38.1 us
  Pallas kernels  35.1 us (92%)
  local copies, waits for them, and re-layouts  1.71 us (4%)
  between operations  1.29 us (3%)
    pallas_call x1, Pallas kernels, shards(): pl.pallas_call(functools.partial(kernel, ncols, nchan), out_shape=(jax.Sh...  35.1 us
    unnamed x1, local copies, waits for them, and re-layouts  1.06 us

profile of v2, /device:TPU:5, one launch (start us, length us, event | category | flops | bytes accessed | tf_op | source)
XLA Modules:
  0.0 38.1 jit_solution(12866933146366582218)
XLA Ops:
  1.3 35.1 %shard_map.77 = (bf16[80,64,128]{2,1,0:T(8,128)(2,1)S(1)}, f32[8,20,80]{2,1,0:T(8,128)S(1)}) custom-call(bf16[256,80,128]{2,1,0:T(8,128)(2,1)} %anom.1, bf16[32,256,128]{2,1,0:T(8,128)(2,1)} %jac.1, s32[4,128]{1,0:T(4,128)} %bitcast.4, f32[4,128]{1,0:T(4,128)} %bitcast.5, bf16[32,256]{1,0:T(8,128)(2,1)} %bitcast.3, s32[1]{0:T(128)S(6)} %copy.10.cnt_s), custom_call_target="tpu_custom_call" | custom-call | tf_op jit(solution)/shard_map/pallas_call | solution.py:268
  36.4 0.7 %copy.8 = f32[8,20,80]{2,0,1:T(8,128)} copy(f32[8,20,80]{2,1,0:T(8,128)S(1)} %get-tuple-element.3) | data formatting | bytes 102400 | tf_op jit(solution)/shard_map/pallas_call | solution.py:268
  37.0 1.1 %copy.11 = bf16[80,64,128]{2,1,0:T(8,128)(2,1)} copy(bf16[80,64,128]{2,1,0:T(8,128)(2,1)S(1)} %get-tuple-element.6) | data formatting | bytes 2621440

commit v3 on v2

--- a/solution.py
+++ b/solution.py
@@ -10,7 +10,7 @@
 HALO = 32
 PTS = 8
 LANES = 128
-ROWS = 16
+ROWS = 8
 MESH = pl.DeviceIdType.MESH
 
 
@@ -174,7 +174,7 @@
                 stage[q, pl.ds(n, group, stride=obs), :] = piece
             return carry
 
-        lax.fori_loop(0, obs, one, 0, unroll=4)
+        lax.fori_loop(0, obs, one, 0, unroll=16)
         for q in range(nchan):
             sbuf[k, q] = stage[q].astype(jnp.bfloat16).reshape(group, obs, LANES)
         place = pl.ds(pl.multiple_of(first, obs), obs)
@@ -204,7 +204,7 @@
         )
         return carry
 
-    lax.fori_loop(0, obs, product, 0, unroll=4)
+    lax.fori_loop(0, obs, product, 0, unroll=16)
 
     def point(p, carry):
         sums = [None, None]

time: 38.2 us -> 36.8 us (0.963)
  Pallas kernels: 35.1 us -> 33.6 us
    pallas_call x1, Pallas kernels: 35.1 us -> 33.6 us  [shards(): pl.pallas_call(functools.partial(kernel, ncols, nchan), out_shape=(jax.Sh...]
where the time goes in v3:
time: 36.8 us; the launch traced here: 36.6 us
  Pallas kernels  33.6 us (91%)
  local copies, waits for them, and re-layouts  1.71 us (5%)
  between operations  1.29 us (4%)
    pallas_call x1, Pallas kernels, shards(): pl.pallas_call(functools.partial(kernel, ncols, nchan), out_shape=(jax.Sh...  33.6 us
    unnamed x1, local copies, waits for them, and re-layouts  1.06 us

profile of v3, /device:TPU:5, one launch (start us, length us, event | category | flops | bytes accessed | tf_op | source)
XLA Modules:
  0.0 36.6 jit_solution(5947055378603035856)
XLA Ops:
  1.3 33.6 %shard_map.77 = (bf16[80,64,128]{2,1,0:T(8,128)(2,1)S(1)}, f32[8,20,80]{2,1,0:T(8,128)S(1)}) custom-call(bf16[256,80,128]{2,1,0:T(8,128)(2,1)} %anom.1, bf16[32,256,128]{2,1,0:T(8,128)(2,1)} %jac.1, s32[4,128]{1,0:T(4,128)} %bitcast.4, f32[4,128]{1,0:T(4,128)} %bitcast.5, bf16[32,256]{1,0:T(8,128)(2,1)} %bitcast.3, s32[1]{0:T(128)S(6)} %copy.10.cnt_s), custom_call_target="tpu_custom_call" | custom-call | tf_op jit(solution)/shard_map/pallas_call | solution.py:268
  34.9 0.7 %copy.8 = f32[8,20,80]{2,0,1:T(8,128)} copy(f32[8,20,80]{2,1,0:T(8,128)S(1)} %get-tuple-element.3) | data formatting | bytes 102400 | tf_op jit(solution)/shard_map/pallas_call | solution.py:268
  35.6 1.1 %copy.11 = bf16[80,64,128]{2,1,0:T(8,128)(2,1)} copy(bf16[80,64,128]{2,1,0:T(8,128)(2,1)S(1)} %get-tuple-element.6) | data formatting | bytes 2621440
